TPU v7x, 32 devices: a whole 2x2x4 slice. The times are simulated.
32 devices in a mesh: groups: 2 (over y), gx: 16 (over z, x, core).
Axes of the slice: x: 2, y: 2, z: 4, core: 2. Of those that a mesh axis runs over, the one named last changes fastest.
Arguments:
- grad_out: bfloat16 [64, 4, 128, 128], P(('groups', 'gx')), parts along dimension 0, may hold values from -6 to 6
- inputs: bfloat16 [64, 4, 128, 128], P(('groups', 'gx')), parts along dimension 0, may hold values from -6 to 6
- pre_first: bfloat16 [64, 4, 128, 128], P(('groups', 'gx')), parts along dimension 0, may hold values from -6 to 6
- pre_second: bfloat16 [64, 4, 128, 128], P(('groups', 'gx')), parts along dimension 0, may hold values from -6 to 6
- filter_first: bfloat16 [3456, 128], P('gx'), may hold values from -0.109375 to 0.109375
- filter_second: bfloat16 [3456, 128], P('gx'), may hold values from -0.109375 to 0.109375
Outputs:
- grad_inputs: bfloat16 [64, 4, 128, 128], P(('groups', 'gx')), parts along dimension 0
- grad_filter_first: float32 [3456, 256], P('gx', 'groups'), parts along dimension 1
- grad_filter_second: float32 [3456, 256], P('gx', 'groups'), parts along dimension 1
There are 2 independent parts, one for each index of `groups`. A program takes and returns all parts, laid end to end along the dimension named above; an argument that names none is the same for every part. Nothing has to cross between parts.
All inputs are finite; a program needn't handle non-finite values.
Results may differ from a plain program's by a relative error of at most 0.0058.
Values may be sent and summed in bfloat16 or wider, within the bound.
A program may use at most 64 MiB of HBM per device.

v0:
```python
import math

import jax
import jax.numpy as jnp
from jax import lax
from jax.sharding import PartitionSpec as P

inv_root_two = 0.7071067811865476
inv_root_twopi = 0.3989422804014327
tap_shifts = ((-1, -1), (-1, 0), (-1, 1), (0, -1), (0, 0), (0, 1), (1, -1), (1, 0), (1, 1))


def with_halo(block, sides, width):
    for axis, dim in sides:
        count = lax.axis_size(axis)
        forward = [(i, i + 1) for i in range(count - 1)]
        backward = [(target, source) for source, target in forward]
        low = lax.ppermute(
            lax.slice_in_dim(block, block.shape[dim] - width, None, axis=dim), axis, forward
        )
        high = lax.ppermute(lax.slice_in_dim(block, 0, width, axis=dim), axis, backward)
        block = jnp.concatenate([low, block, high], axis=dim)
    return block


def gelu_parts(value):
    normal_cdf = 0.5 * (1.0 + lax.erf(value * inv_root_two))
    return (value * normal_cdf, normal_cdf + value * jnp.exp(-0.5 * value * value) * inv_root_twopi)


def pad_sides(extended):
    return jnp.pad(extended, ((0, 0), (1, 1), (1, 1), (0, 0)))


def stack_taps(padded, direction, z_cells):
    return jnp.concatenate(
        [
            padded[:, :, 1 + direction * shift_z : 1 + direction * shift_z + z_cells]
            for shift_z in (-1, 0, 1)
        ],
        axis=3,
    )


def window(stacked, direction, shift_x, shift_y, x_cells, y_cells):
    start_x = 1 + direction * shift_x
    start_y = 1 + direction * shift_y
    return stacked[start_x : start_x + x_cells, start_y : start_y + y_cells]


def back_data(stacked, full_filter, shape):
    x_cells, y_cells, z_cells, channels = shape
    kernel = full_filter.reshape(3, 3, 3, channels, channels)
    running = jnp.zeros((x_cells * y_cells * z_cells, channels), jnp.float32)
    for shift_x, shift_y in tap_shifts:
        tap_matrix = jnp.transpose(kernel[shift_x + 1, shift_y + 1], (0, 2, 1)).reshape(
            3 * channels, channels
        )
        piece = window(stacked, -1, shift_x, shift_y, x_cells, y_cells).reshape(-1, 3 * channels)
        running = running + jnp.dot(piece, tap_matrix, preferred_element_type=jnp.float32)
    return running.reshape(shape)


def filter_from_inputs(stacked, grads, shape):
    x_cells, y_cells, z_cells, channels = shape
    flat_grads = grads.reshape(-1, channels)
    blocks = []
    for shift_x, shift_y in tap_shifts:
        piece = window(stacked, 1, shift_x, shift_y, x_cells, y_cells).reshape(-1, 3 * channels)
        product = lax.dot_general(
            piece, flat_grads, (((0,), (0,)), ((), ())), preferred_element_type=jnp.float32
        )
        blocks.append(product.reshape(3, channels, channels))
    return jnp.stack(blocks).reshape(27 * channels, channels)


def on_device(grad_out, inputs, pre_first, pre_second, filter_first, filter_second):
    shape = grad_out.shape
    x_cells, y_cells, z_cells, channels = shape
    full_first, full_second = (
        lax.all_gather(filter_first, "gx", axis=0, tiled=True),
        lax.all_gather(filter_second, "gx", axis=0, tiled=True),
    )
    grad_scale = 1.0 / math.sqrt(x_cells * lax.axis_size("gx") * y_cells * z_cells)
    unused_value, slope_two = gelu_parts(pre_second.astype(jnp.float32))
    grad_two = (grad_out.astype(jnp.float32) * slope_two).astype(jnp.bfloat16)
    act_one, slope_one = gelu_parts(pre_first.astype(jnp.float32))
    act_one = act_one.astype(jnp.bfloat16)
    extended_two = pad_sides(with_halo(grad_two, (("gx", 0),), 1))
    stacked_two = stack_taps(extended_two, -1, z_cells)
    grad_act = back_data(stacked_two, full_second, shape)
    extended_act = pad_sides(with_halo(act_one, (("gx", 0),), 1))
    filt_two = filter_from_inputs(stack_taps(extended_act, 1, z_cells), grad_two, shape)
    owned_two = lax.psum_scatter(filt_two * grad_scale, "gx", scatter_dimension=0, tiled=True)
    grad_one = (grad_act * slope_one).astype(jnp.bfloat16)
    extended_one = pad_sides(with_halo(grad_one, (("gx", 0),), 1))
    stacked_one = stack_taps(extended_one, -1, z_cells)
    grad_in = back_data(stacked_one, full_first, shape).astype(jnp.bfloat16)
    extended_in = pad_sides(with_halo(inputs, (("gx", 0),), 1))
    filt_one = filter_from_inputs(stack_taps(extended_in, 1, z_cells), grad_one, shape)
    owned_one = lax.psum_scatter(filt_one * grad_scale, "gx", scatter_dimension=0, tiled=True)
    return (grad_in, owned_one, owned_two)


def solution(mesh):
    return jax.shard_map(
        on_device,
        mesh=mesh,
        in_specs=(
            P(("groups", "gx"), None, None, None),
            P(("groups", "gx"), None, None, None),
            P(("groups", "gx"), None, None, None),
            P(("groups", "gx"), None, None, None),
            P("gx", None),
            P("gx", None),
        ),
        out_specs=(P(("groups", "gx"), None, None, None), P("gx", "groups"), P("gx", "groups")),
        check_vma=False,
    )
```

profile of v0, /device:TPU:0, one launch (start us, length us, event | category | flops | bytes accessed | tf_op | source)
XLA Modules:
  0.0 240.3 jit_solution(2197010658242407389)
XLA Ops:
  8.5 2.4 %collective-permute-start = (bf16[1,4,128,128]{3,2,1,0:T(8,128)(2,1)S(1)}, bf16[1,4,128,128]{3,2,1,0:T(8,128)(2,1)S(1)}, u32[]{:S(2)}, u32[]{:S(2)}) collective-permute-start(bf16[1,4,128,128]{3,2,1,0:T(8,128)(2,1)S(1)} %get-tuple-element.77), channel_id=1, source_target_pairs={{0,1},{1,2},{2,3},{3,4},{4,5},{5,6},{6,7},{7,8},{8,9},{9,10},{10,1... | collective-permute-start | bytes 393224 | tf_op jit(solution)/shard_map/ppermute | solution.py:18
  13.2 5.1 %collective-permute-start.4 = (bf16[1,4,128,128]{3,2,1,0:T(8,128)(2,1)S(1)}, bf16[1,4,128,128]{3,2,1,0:T(8,128)(2,1)S(1)}, u32[]{:S(2)}, u32[]{:S(2)}) collective-permute-start(bf16[1,4,128,128]{3,2,1,0:T(8,128)(2,1)S(1)} %get-tuple-element.73), channel_id=1, source_target_pairs={{0,1},{1,2},{2,3},{3,4},{4,5},{5,6},{6,7},{7,8},{8,9},{9,10},{10,1... | collective-permute-start | bytes 393224 | tf_op jit(solution)/shard_map/ppermute | solution.py:18
  19.7 26.8 %all_gather.6 = bf16[3456,128]{1,0:T(8,128)(2,1)S(1)} all-gather(bf16[216,128]{1,0:T(8,128)(2,1)S(1)} %copy-done.16), channel_id=1, replica_groups=mesh['groups'=2,'gx'=16] {'gx'}, dimensions={0}, use_global_device_ids=true | all-gather | bytes 940032 | tf_op jit(solution)/shard_map/all_gather | solution.py:82
  47.8 19.9 %all_gather.7 = bf16[3456,128]{1,0:T(8,128)(2,1)S(1)} all-gather(bf16[216,128]{1,0:T(8,128)(2,1)S(1)} %copy-done.17), channel_id=1, replica_groups=mesh['groups'=2,'gx'=16] {'gx'}, dimensions={0}, use_global_device_ids=true | all-gather | bytes 940032 | tf_op jit(solution)/shard_map/all_gather | solution.py:81
  78.9 2.9 %collective-permute-start.6 = (bf16[1,4,128,128]{3,2,1,0:T(8,128)(2,1)}, bf16[1,4,128,128]{3,2,1,0:T(8,128)(2,1)}, u32[]{:S(2)}, u32[]{:S(2)}) collective-permute-start(bf16[1,4,128,128]{3,2,1,0:T(8,128)(2,1)} %get-tuple-element.69), channel_id=1, source_target_pairs={{0,1},{1,2},{2,3},{3,4},{4,5},{5,6},{6,7},{7,8},{8,9},{9,10},{10,1... | collective-permute-start | bytes 393224 | tf_op jit(solution)/shard_map/ppermute | solution.py:18
  84.4 2.8 %fusion.48 = (bf16[2,4,128,384]{3,2,1,0:T(8,128)(2,1)S(1)}, bf16[2,4,128,384]{3,2,1,0:T(8,128)(2,1)S(1)}, bf16[2,4,128,384]{3,2,1,0:T(8,128)(2,1)S(1)}, bf16[2,4...) fusion(bf16[4,6,128,384]{3,2,1,0:T(8,128)(2,1)S(1)} %pad_maximu, ...), kind=kLoop, calls=%fused_computation.125 | loop fusion | bytes 14155776 | tf_op jit(solution)/shard_map/slice | solution.py:48
  87.2 2.3 copy.99
  89.6 2.3 copy.100
  91.9 2.3 copy.101
  94.2 2.3 copy.102
  96.5 2.3 copy.103
  98.8 2.3 copy.104
  111.0 4.1 %collective-permute-start.2 = (bf16[1,4,128,128]{3,2,1,0:T(8,128)(2,1)}, bf16[1,4,128,128]{3,2,1,0:T(8,128)(2,1)}, u32[]{:S(2)}, u32[]{:S(2)}) collective-permute-start(bf16[1,4,128,128]{3,2,1,0:T(8,128)(2,1)} %get-tuple-element.75), channel_id=1, source_target_pairs={{0,1},{1,2},{2,3},{3,4},{4,5},{5,6},{6,7},{7,8},{8,9},{9,10},{10,1... | collective-permute-start | bytes 393224 | tf_op jit(solution)/shard_map/ppermute | solution.py:18
  118.7 2.8 %fusion.47 = (bf16[2,4,128,384]{3,2,1,0:T(8,128)(2,1)S(1)}, bf16[2,4,128,384]{3,2,1,0:T(8,128)(2,1)S(1)}, bf16[2,4,128,384]{3,2,1,0:T(8,128)(2,1)S(1)}, bf16[2,4...) fusion(bf16[4,6,128,384]{3,2,1,0:T(8,128)(2,1)S(1)} %pad_maximu, ...), kind=kLoop, calls=%fused_computation.124 | loop fusion | bytes 14155776 | tf_op jit(solution)/shard_map/slice | solution.py:48
  121.5 2.4 copy.108
  123.9 2.3 copy.109
  130.6 2.4 copy.110
  133.0 2.3 copy.111
  135.3 2.3 copy.112
  137.6 2.3 copy.113
  143.0 2.3 fusion.10
  152.1 2.9 %broadcast_multiply_fusion = f32[9,3,128,128]{3,2,1,0:T(8,128)} fusion(f32[9,3,128,128]{3,2,1,0:T(8,128)} %fusion.4), kind=kLoop, calls=%fused_computation.73 | loop fusion | flops 442368 | bytes 3538944 | tf_op jit(solution)/shard_map/mul | solution.py:94
  160.9 10.2 %reduce-scatter.7.cloned.1.call-done = f32[216,128]{1,0:T(8,128)} async-done(((f32[3456,128]{1,0:T(8,128)}), f32[216,128]{1,0:T(8,128)}) %reduce-scatter.7.cloned.1.call-update) | async-done | bytes 110608
  171.1 62.3 %reduce-scatter.9.cloned.1.call-done = f32[216,128]{1,0:T(8,128)} async-done(((f32[3456,128]{1,0:T(8,128)}), f32[216,128]{1,0:T(8,128)}) %reduce-scatter.9.cloned.1.call-update) | async-done | bytes 110608
  (134 shorter events, 53.1 us)
Async XLA Ops:
  7.2 12.5 %copy-start.16 = (bf16[216,128]{1,0:T(8,128)(2,1)S(1)}, bf16[216,128]{1,0:T(8,128)(2,1)}, u32[]{:S(2)}) copy-start(bf16[216,128]{1,0:T(8,128)(2,1)} %param.11) | copy-start | bytes 165892
  7.2 163.9 %reduce-scatter.7.cloned.1.call-start = ((), (), s32[]{:S(2)}) async-start(), calls=%async_computation.2 | async-start | bytes 1880064
  8.5 63.5 %collective-permute-start = (bf16[1,4,128,128]{3,2,1,0:T(8,128)(2,1)S(1)}, bf16[1,4,128,128]{3,2,1,0:T(8,128)(2,1)S(1)}, u32[]{:S(2)}, u32[]{:S(2)}) collective-permute-start(bf16[1,4,128,128]{3,2,1,0:T(8,128)(2,1)S(1)} %get-tuple-element.77), channel_id=1, source_target_pairs={{0,1},{1,2},{2,3},{3,4},{4,5},{5,6},{6,7},{7,8},{8,9},{9,10},{10,1... | collective-permute-start | bytes 393224 | tf_op jit(solution)/shard_map/ppermute | solution.py:18
  11.0 61.1 %collective-permute-start.1 = (bf16[1,4,128,128]{3,2,1,0:T(8,128)(2,1)S(1)}, bf16[1,4,128,128]{3,2,1,0:T(8,128)(2,1)S(1)}, u32[]{:S(2)}, u32[]{:S(2)}) collective-permute-start(bf16[1,4,128,128]{3,2,1,0:T(8,128)(2,1)S(1)} %get-tuple-element.78), channel_id=1, source_target_pairs={{1,0},{2,1},{3,2},{4,3},{5,4},{6,5},{7,6},{8,7},{9,8},{10,9},{11,1... | collective-permute-start | bytes 393224 | tf_op jit(solution)/shard_map/ppermute | solution.py:21
  13.2 70.1 %collective-permute-start.4 = (bf16[1,4,128,128]{3,2,1,0:T(8,128)(2,1)S(1)}, bf16[1,4,128,128]{3,2,1,0:T(8,128)(2,1)S(1)}, u32[]{:S(2)}, u32[]{:S(2)}) collective-permute-start(bf16[1,4,128,128]{3,2,1,0:T(8,128)(2,1)S(1)} %get-tuple-element.73), channel_id=1, source_target_pairs={{0,1},{1,2},{2,3},{3,4},{4,5},{5,6},{6,7},{7,8},{8,9},{9,10},{10,1... | collective-permute-start | bytes 393224 | tf_op jit(solution)/shard_map/ppermute | solution.py:18
  18.4 64.9 %collective-permute-start.5 = (bf16[1,4,128,128]{3,2,1,0:T(8,128)(2,1)S(1)}, bf16[1,4,128,128]{3,2,1,0:T(8,128)(2,1)S(1)}, u32[]{:S(2)}, u32[]{:S(2)}) collective-permute-start(bf16[1,4,128,128]{3,2,1,0:T(8,128)(2,1)S(1)} %get-tuple-element.74), channel_id=1, source_target_pairs={{1,0},{2,1},{3,2},{4,3},{5,4},{6,5},{7,6},{8,7},{9,8},{10,9},{11,1... | collective-permute-start | bytes 393224 | tf_op jit(solution)/shard_map/ppermute | solution.py:21
  46.5 1.3 copy-start.17
  77.3 6.0 %copy-start.9 = (bf16[2,4,128,128]{3,2,1,0:T(8,128)(2,1)S(1)}, bf16[2,4,128,128]{3,2,1,0:T(8,128)(2,1)}, u32[]{:S(2)}) copy-start(bf16[2,4,128,128]{3,2,1,0:T(8,128)(2,1)} %param.7) | copy-start | bytes 786436
  78.9 37.7 %collective-permute-start.6 = (bf16[1,4,128,128]{3,2,1,0:T(8,128)(2,1)}, bf16[1,4,128,128]{3,2,1,0:T(8,128)(2,1)}, u32[]{:S(2)}, u32[]{:S(2)}) collective-permute-start(bf16[1,4,128,128]{3,2,1,0:T(8,128)(2,1)} %get-tuple-element.69), channel_id=1, source_target_pairs={{0,1},{1,2},{2,3},{3,4},{4,5},{5,6},{6,7},{7,8},{8,9},{9,10},{10,1... | collective-permute-start | bytes 393224 | tf_op jit(solution)/shard_map/ppermute | solution.py:18
  81.8 34.8 %collective-permute-start.7 = (bf16[1,4,128,128]{3,2,1,0:T(8,128)(2,1)}, bf16[1,4,128,128]{3,2,1,0:T(8,128)(2,1)}, u32[]{:S(2)}, u32[]{:S(2)}) collective-permute-start(bf16[1,4,128,128]{3,2,1,0:T(8,128)(2,1)} %get-tuple-element.70), channel_id=1, source_target_pairs={{1,0},{2,1},{3,2},{4,3},{5,4},{6,5},{7,6},{8,7},{9,8},{10,9},{11,1... | collective-permute-start | bytes 393224 | tf_op jit(solution)/shard_map/ppermute | solution.py:21
  102.9 3.2 %copy-start.8 = (bf16[1024,384]{0,1:T(8,128)(2,1)S(1)}, bf16[1024,384]{0,1:T(8,128)(2,1)}, u32[]{:S(2)}) copy-start(bf16[1024,384]{0,1:T(8,128)(2,1)} %copy.101) | copy-start | bytes 2359300
  102.9 3.6 %copy-start.7 = (bf16[1024,384]{0,1:T(8,128)(2,1)S(1)}, bf16[1024,384]{0,1:T(8,128)(2,1)}, u32[]{:S(2)}) copy-start(bf16[1024,384]{0,1:T(8,128)(2,1)} %copy.102) | copy-start | bytes 2359300
  104.5 2.4 copy-start.6
  106.1 1.2 copy-start.5
  106.5 1.2 copy-start.4
  110.3 123.1 %reduce-scatter.9.cloned.1.call-start = ((), (), s32[]{:S(2)}) async-start(), calls=%async_computation.3 | async-start | bytes 1880064
  111.0 30.7 %collective-permute-start.2 = (bf16[1,4,128,128]{3,2,1,0:T(8,128)(2,1)}, bf16[1,4,128,128]{3,2,1,0:T(8,128)(2,1)}, u32[]{:S(2)}, u32[]{:S(2)}) collective-permute-start(bf16[1,4,128,128]{3,2,1,0:T(8,128)(2,1)} %get-tuple-element.75), channel_id=1, source_target_pairs={{0,1},{1,2},{2,3},{3,4},{4,5},{5,6},{6,7},{7,8},{8,9},{9,10},{10,1... | collective-permute-start | bytes 393224 | tf_op jit(solution)/shard_map/ppermute | solution.py:18
  115.1 26.6 %collective-permute-start.3 = (bf16[1,4,128,128]{3,2,1,0:T(8,128)(2,1)}, bf16[1,4,128,128]{3,2,1,0:T(8,128)(2,1)}, u32[]{:S(2)}, u32[]{:S(2)}) collective-permute-start(bf16[1,4,128,128]{3,2,1,0:T(8,128)(2,1)} %get-tuple-element.76), channel_id=1, source_target_pairs={{1,0},{2,1},{3,2},{4,3},{5,4},{6,5},{7,6},{8,7},{9,8},{10,9},{11,1... | collective-permute-start | bytes 393224 | tf_op jit(solution)/shard_map/ppermute | solution.py:21
  141.7 3.6 %copy-start.3 = (bf16[1024,384]{0,1:T(8,128)(2,1)S(1)}, bf16[1024,384]{0,1:T(8,128)(2,1)}, u32[]{:S(2)}) copy-start(bf16[1024,384]{0,1:T(8,128)(2,1)} %copy.111) | copy-start | bytes 2359300
  141.7 4.6 %copy-start.2 = (bf16[1024,384]{0,1:T(8,128)(2,1)S(1)}, bf16[1024,384]{0,1:T(8,128)(2,1)}, u32[]{:S(2)}) copy-start(bf16[1024,384]{0,1:T(8,128)(2,1)} %copy.112) | copy-start | bytes 2359300
  143.0 4.4 %copy-start.1 = (bf16[1024,384]{0,1:T(8,128)(2,1)S(1)}, bf16[1024,384]{0,1:T(8,128)(2,1)}, u32[]{:S(2)}) copy-start(bf16[1024,384]{0,1:T(8,128)(2,1)} %copy.113) | copy-start | bytes 2359300
  145.2 3.1 %copy-start = (bf16[1024,384]{0,1:T(8,128)(2,1)S(1)}, bf16[1024,384]{0,1:T(8,128)(2,1)}, u32[]{:S(2)}) copy-start(bf16[1024,384]{0,1:T(8,128)(2,1)} %copy.114) | copy-start | bytes 2359300
  155.4 1.2 copy-start.14
  155.4 1.6 copy-start.13
  (4 other events, 3.7 us)
Sparse Core Ops, SparseCore 0:
  110.4 60.6 reduce-scatter.6
  175.4 57.9 reduce-scatter.8
where the time goes:
time: 241 us; the launch traced here: 240 us
  waiting for transfers between devices  72.6 us (30%)
  local copies, waits for them, and re-layouts  49.9 us (21%)
  blocking collectives  46.8 us (19%)
  matrix products  26 us (11%)
  starting transfers between devices  20.1 us (8%)
  between operations  14.8 us (6%)
  other arithmetic  10.1 us (4%)
    unnamed x4, waiting for transfers between devices  72.5 us
    reshape x18, local copies, waits for them, and re-layouts, filter_from_inputs(): window(stacked, 1, shift_x, shift_y, x_cells, y_cells)  31.4 us
    all_gather x1, blocking collectives, on_device(): lax.all_gather(filter_second, 'gx', axis=0, tiled=True)  26.8 us
    all_gather x1, blocking collectives, on_device(): lax.all_gather(filter_first, 'gx', axis=0, tiled=True)  19.9 us
    dot_general x18, matrix products, filter_from_inputs(): lax.dot_general(piece, flat_grads, (((0,), (0,)), ((), ())), preferred_el...  18.7 us
    ppermute x4, starting transfers between devices, with_halo(): lax.ppermute(lax.slice_in_dim(block, block.shape[dim] - width, None, axis...  14.5 us
    slice x4, local copies, waits for them, and re-layouts, window(): return stacked[start_x:start_x + x_cells, start_y:start_y + y_cells]  7.85 us
    dot_general x18, matrix products, back_data(): jnp.dot(piece, tap_matrix, preferred_element_type=jnp.float32)  7.26 us
  transfers between devices with their start and end apart: 10, of which 2 were waited for; matrix products, arithmetic and copies ran while one was open for 35% of the time, Pallas kernels for 0%

commit v1 on v0

--- a/solution.py
+++ b/solution.py
@@ -1,8 +1,11 @@
+import functools
 import math
 
 import jax
 import jax.numpy as jnp
 from jax import lax
+from jax.experimental import pallas as pl
+from jax.experimental.pallas import tpu as pltpu
 from jax.sharding import PartitionSpec as P
 
 inv_root_two = 0.7071067811865476
@@ -102,9 +105,366 @@
     return (grad_in, owned_one, owned_two)
 
 
+MESH = pl.DeviceIdType.MESH
+sub = 8
+
+
+def shift_z(block, shift):
+    if shift == 0:
+        return block
+    cells = block.shape[0]
+    row = lax.broadcasted_iota(jnp.int32, block.shape, 0)
+    edge = 0 if shift > 0 else cells - 1
+    return jnp.where(row == edge, 0.0, pltpu.roll(block, shift % cells, 0))
+
+
+def kernel(
+    n, go, xin, p1, p2, f1, f2, gin, own1, own2,
+    fbuf, wbuf, gext, abuf, ahalo, sat, gcat, slope, part, s1, r1, s2, r2, s3, r3,
+    halo_s, halo_r, agz_s, agz_r, agx_s, agx_r, agc_s, agc_r,
+    rs1_s, rs1_r, rs2_s, rs2_r, rs3_s, rs3_r,
+):
+    xs, ys, zs, ch = go.shape
+    units = f1.shape[0]
+    hi = n // 4
+    group, me = lax.axis_index("groups"), lax.axis_index("gx")
+    core = me % 2
+    mid = (me // 2) % 2
+    top = me // 4
+    partner = me + 1 - 2 * core
+    across = me + 2 - 4 * mid
+
+    def owner(t, m, c):
+        return (t * 2 + m) * 2 + c
+
+    def chunk(t, m, c):
+        return pl.ds(owner(t, m, c) * units, units)
+
+    def ahead(d):
+        return lax.rem(top + d, hi)
+
+    def behind(d):
+        return lax.rem(top + hi - d, hi)
+
+    sent = []
+
+    def push(src, dst, send, recv, target):
+        copy = pltpu.make_async_remote_copy(
+            src_ref=src, dst_ref=dst, send_sem=send, recv_sem=recv,
+            device_id=(group, target), device_id_type=MESH,
+        )
+        copy.start()
+        sent.append(copy)
+
+    def arrive(dst, send, recv):
+        pltpu.make_async_remote_copy(
+            src_ref=dst, dst_ref=dst, send_sem=send, recv_sem=recv,
+            device_id=(group, partner), device_id_type=MESH,
+        ).wait_recv()
+
+    barrier = pltpu.get_barrier_semaphore()
+    peers = [partner, across, lax.rem(me + 1, n), lax.rem(me + n - 1, n)]
+    peers += [owner(ahead(d), mid, core) for d in range(1, hi)]
+    for peer in peers:
+        pl.semaphore_signal(barrier, inc=1, device_id=(group, peer), device_id_type=MESH)
+    pl.semaphore_wait(barrier, len(peers))
+
+    filters = (f2, f1)
+
+    def gather_own(f):
+        mine = fbuf.at[f, chunk(top, mid, core)]
+        for d in range(1, hi):
+            push(filters[f], mine, agz_s.at[f, d], agz_r.at[f, d], owner(ahead(d), mid, core))
+        push(filters[f], mine, agx_s.at[f, 0], agx_r.at[f, 0], across)
+        push(filters[f], mine, agc_s.at[f, 0], agc_r.at[f, 0], partner)
+        fbuf[f, chunk(top, mid, core)] = filters[f][...]
+
+    def gather_top(f):
+        for d in range(1, hi):
+            got = fbuf.at[f, chunk(behind(d), mid, core)]
+            arrive(got, agz_s.at[f, d], agz_r.at[f, d])
+            push(got, got, agx_s.at[f, d], agx_r.at[f, d], across)
+            push(got, got, agc_s.at[f, d], agc_r.at[f, d], partner)
+
+    def gather_mid(f):
+        for d in range(hi):
+            got = fbuf.at[f, chunk(behind(d), 1 - mid, core)]
+            arrive(got, agx_s.at[f, d], agx_r.at[f, d])
+            push(got, got, agc_s.at[f, hi + d], agc_r.at[f, hi + d], partner)
+
+    def gather_core(f):
+        for m in range(2):
+            for d in range(hi):
+                which = mid if m == 0 else 1 - mid
+                got = fbuf.at[f, chunk(behind(d), which, 1 - core)]
+                arrive(got, agc_s.at[f, m * hi + d], agc_r.at[f, m * hi + d])
+        taps = 3 * ch // sub
+        for ab in range(9):
+            rows = fbuf[f, ab * taps : (ab + 1) * taps].astype(jnp.float32)
+            wbuf[f, :, ab * ch : (ab + 1) * ch] = rows.reshape(3 * ch, ch).astype(jnp.bfloat16)
+
+    def halo_copy(h, first, last, low, high):
+        to_left = pltpu.make_async_remote_copy(
+            src_ref=first, dst_ref=high, send_sem=halo_s.at[h, 0], recv_sem=halo_r.at[h, 1],
+            device_id=(group, lax.rem(me + n - 1, n)), device_id_type=MESH,
+        )
+        to_right = pltpu.make_async_remote_copy(
+            src_ref=last, dst_ref=low, send_sem=halo_s.at[h, 1], recv_sem=halo_r.at[h, 0],
+            device_id=(group, lax.rem(me + 1, n)), device_id_type=MESH,
+        )
+
+        @pl.when(me > 0)
+        def _():
+            to_left.start()
+
+        @pl.when(me < n - 1)
+        def _():
+            to_right.start()
+
+        return to_left, to_right, low, high, h
+
+    def halo_wait(halo):
+        _, _, low, high, h = halo
+
+        @pl.when(me > 0)
+        def _():
+            arrive(low, halo_s.at[h, 0], halo_r.at[h, 0])
+
+        @pl.when(me == 0)
+        def _():
+            low[...] = jnp.zeros(low.shape, low.dtype)
+
+        @pl.when(me < n - 1)
+        def _():
+            arrive(high, halo_s.at[h, 1], halo_r.at[h, 1])
+
+        @pl.when(me == n - 1)
+        def _():
+            high[...] = jnp.zeros(high.shape, high.dtype)
+
+    def grad_halo(h, f):
+        inner = pl.ds(1, ys)
+        return halo_copy(
+            h, gext.at[f, 1, inner], gext.at[f, xs, inner],
+            gext.at[f, 0, inner], gext.at[f, xs + 1, inner],
+        )
+
+    def saved_halo(h, s, block):
+        return halo_copy(h, block.at[0], block.at[xs - 1], ahalo.at[s, 0], ahalo.at[s, 1])
+
+    def keep_grad(f, x, y, value):
+        gext[f, x + 1, y + 1] = value.astype(jnp.bfloat16)
+        start = pl.multiple_of((x * ys + y) * zs, zs)
+        for c in (-1, 0, 1):
+            gcat[f, pl.ds(start, zs), (c + 1) * ch : (c + 2) * ch] = shift_z(value, c).astype(
+                jnp.bfloat16
+            )
+
+    def turn(s, layer, block):
+        for y in range(ys):
+            sat[s, layer, :, (y + 1) * zs : (y + 2) * zs] = block[y].T
+
+    def filter_terms(s):
+        for a in range(3):
+            lhs = jnp.concatenate(
+                [
+                    jnp.concatenate(
+                        [sat[s, x + a, :, b * zs : (b + ys) * zs] for x in range(xs)], axis=1
+                    )
+                    for b in range(3)
+                ],
+                axis=0,
+            )
+            out = jnp.dot(lhs, gcat[s], preferred_element_type=jnp.float32)
+            per = ch // sub
+            for b in range(3):
+                for c in range(3):
+                    at = (9 * a + 3 * b + c) * per
+                    part[s, at : at + per] = out[
+                        b * ch : (b + 1) * ch, c * ch : (c + 1) * ch
+                    ].reshape(per, sub, ch)
+
+    def scatter_core(s):
+        for m in range(2):
+            which = 1 - mid if m == 0 else mid
+            for t in range(hi):
+                s1[s, m, t] = part[s, chunk(t, which, 1 - core)].astype(jnp.bfloat16)
+            push(s1.at[s, m], r1.at[s, m], rs1_s.at[s, m], rs1_r.at[s, m], partner)
+
+    def scatter_mid(s):
+        arrive(r1.at[s, 0], rs1_s.at[s, 0], rs1_r.at[s, 0])
+        for t in range(hi):
+            s2[s, t] = (
+                part[s, chunk(t, 1 - mid, core)] + r1[s, 0, t].astype(jnp.float32)
+            ).astype(jnp.bfloat16)
+        push(s2.at[s], r2.at[s], rs2_s.at[s], rs2_r.at[s], across)
+
+    def total(s, t):
+        return (
+            part[s, chunk(t, mid, core)]
+            + r1[s, 1, t].astype(jnp.float32)
+            + r2[s, t].astype(jnp.float32)
+        )
+
+    def scatter_top(s):
+        arrive(r1.at[s, 1], rs1_s.at[s, 1], rs1_r.at[s, 1])
+        arrive(r2.at[s], rs2_s.at[s], rs2_r.at[s])
+        for d in range(1, hi):
+            s3[s, d] = total(s, ahead(d)).astype(jnp.bfloat16)
+            push(
+                s3.at[s, d], r3.at[s, d], rs3_s.at[s, d], rs3_r.at[s, d],
+                owner(ahead(d), mid, core),
+            )
+
+    def scatter_end(s, out):
+        value = total(s, top)
+        for d in range(1, hi):
+            arrive(r3.at[s, d], rs3_s.at[s, d], rs3_r.at[s, d])
+            value = value + r3[s, d].astype(jnp.float32)
+        out[...] = value * (1.0 / math.sqrt(xs * n * ys * zs))
+
+    def layer_back(f, x):
+        lhs = jnp.concatenate(
+            [
+                gext[f, x + 1 - a, 1 - b : 1 - b + ys].reshape(ys * zs, ch)
+                for a in (-1, 0, 1)
+                for b in (-1, 0, 1)
+            ],
+            axis=1,
+        )
+        wide = lax.dot_general(
+            lhs, wbuf[f], (((1,), (1,)), ((), ())), preferred_element_type=jnp.float32
+        )
+        rows = []
+        for y in range(ys):
+            block = wide[y * zs : (y + 1) * zs]
+            rows.append(
+                shift_z(block[:, :ch], -1) + block[:, ch : 2 * ch] + shift_z(block[:, 2 * ch :], 1)
+            )
+        return rows
+
+    gather_own(0)
+
+    for f in range(2):
+        for x in range(xs + 2):
+            for y in (0, ys + 1):
+                gext[f, x, y] = jnp.zeros((zs, ch), jnp.bfloat16)
+                sat[f, x, :, y * zs : (y + 1) * zs] = jnp.zeros((ch, zs), jnp.bfloat16)
+
+    @pl.loop(0, xs * ys)
+    def _(i):
+        x, y = i // ys, i % ys
+        _, slope_two = gelu_parts(p2[x, y].astype(jnp.float32))
+        keep_grad(0, x, y, go[x, y].astype(jnp.float32) * slope_two)
+        act, slope_one = gelu_parts(p1[x, y].astype(jnp.float32))
+        abuf[x, y] = act.astype(jnp.bfloat16)
+        slope[x, y] = slope_one
+
+    halo_act = saved_halo(0, 0, abuf)
+    halo_two = grad_halo(1, 0)
+    gather_top(0)
+    halo_in = saved_halo(2, 1, xin)
+    gather_own(1)
+    for x in range(xs):
+        turn(0, x + 1, abuf[x])
+        turn(1, x + 1, xin[x])
+    gather_mid(0)
+    halo_wait(halo_act)
+    turn(0, 0, ahalo[0, 0])
+    turn(0, xs + 1, ahalo[0, 1])
+    filter_terms(0)
+    scatter_core(0)
+    gather_top(1)
+    gather_core(0)
+    halo_wait(halo_two)
+    scatter_mid(0)
+    for x in range(xs):
+        for y, value in enumerate(layer_back(0, x)):
+            keep_grad(1, x, y, value * slope[x, y])
+    halo_one = grad_halo(3, 1)
+    gather_mid(1)
+    halo_wait(halo_in)
+    turn(1, 0, ahalo[1, 0])
+    turn(1, xs + 1, ahalo[1, 1])
+    filter_terms(1)
+    scatter_core(1)
+    scatter_top(0)
+    gather_core(1)
+    scatter_mid(1)
+    halo_wait(halo_one)
+    for x in range(xs):
+        for y, value in enumerate(layer_back(1, x)):
+            gin[x, y] = value.astype(jnp.bfloat16)
+        if x == 0:
+            scatter_top(1)
+    scatter_end(0, own2)
+    scatter_end(1, own1)
+    for copy in sent:
+        copy.wait_send()
+    for halo in (halo_act, halo_two, halo_in, halo_one):
+
+        @pl.when(me > 0)
+        def _():
+            halo[0].wait_send()
+
+        @pl.when(me < n - 1)
+        def _():
+            halo[1].wait_send()
+
+
+def fused(grad_out, inputs, pre_first, pre_second, filter_first, filter_second):
+    n = lax.axis_size("gx")
+    xs, ys, zs, ch = grad_out.shape
+    rows = filter_first.shape[0]
+    if rows % sub or n % 4 or n < 8:
+        return on_device(grad_out, inputs, pre_first, pre_second, filter_first, filter_second)
+    units, hi, bf = rows // sub, n // 4, jnp.bfloat16
+    dma = pltpu.SemaphoreType.DMA
+    piece = (units, sub, ch)
+    gin, own1, own2 = pl.pallas_call(
+        functools.partial(kernel, n),
+        out_shape=(
+            jax.ShapeDtypeStruct(grad_out.shape, bf),
+            jax.ShapeDtypeStruct(piece, jnp.float32),
+            jax.ShapeDtypeStruct(piece, jnp.float32),
+        ),
+        in_specs=[pl.BlockSpec(memory_space=pltpu.VMEM)] * 6,
+        out_specs=[pl.BlockSpec(memory_space=pltpu.VMEM)] * 3,
+        scratch_shapes=[
+            pltpu.VMEM((2, n * units, sub, ch), bf),
+            pltpu.VMEM((2, 3 * ch, 9 * ch), bf),
+            pltpu.VMEM((2, xs + 2, ys + 2, zs, ch), bf),
+            pltpu.VMEM((xs, ys, zs, ch), bf),
+            pltpu.VMEM((2, 2, ys, zs, ch), bf),
+            pltpu.VMEM((2, xs + 2, ch, (ys + 2) * zs), bf),
+            pltpu.VMEM((2, xs * ys * zs, 3 * ch), bf),
+            pltpu.VMEM((xs, ys, zs, ch), jnp.float32),
+            pltpu.VMEM((2, n * units, sub, ch), jnp.float32),
+            pltpu.VMEM((2, 2, hi) + piece, bf),
+            pltpu.VMEM((2, 2, hi) + piece, bf),
+            pltpu.VMEM((2, hi) + piece, bf),
+            pltpu.VMEM((2, hi) + piece, bf),
+            pltpu.VMEM((2, hi) + piece, bf),
+            pltpu.VMEM((2, hi) + piece, bf),
+            dma((4, 2)), dma((4, 2)),
+            dma((2, hi)), dma((2, hi)),
+            dma((2, hi)), dma((2, hi)),
+            dma((2, 2 * hi)), dma((2, 2 * hi)),
+            dma((2, 2)), dma((2, 2)),
+            dma((2,)), dma((2,)),
+            dma((2, hi)), dma((2, hi)),
+        ],
+        compiler_params=pltpu.CompilerParams(collective_id=0, has_side_effects=True),
+    )(
+        grad_out, inputs, pre_first, pre_second,
+        filter_first.reshape(piece), filter_second.reshape(piece),
+    )
+    return gin, own1.reshape(rows, ch), own2.reshape(rows, ch)
+
+
 def solution(mesh):
     return jax.shard_map(
-        on_device,
+        fused,
         mesh=mesh,
         in_specs=(
             P(("groups", "gx"), None, None, None),

time: 241 us -> 49.3 us (0.20)
  waiting for transfers between devices: 72.6 us -> 0 us
  blocking collectives: 46.8 us -> 0 us
  local copies, waits for them, and re-layouts: 49.9 us -> 3.29 us
  Pallas kernels: 0 us -> 45.2 us
  matrix products: 26 us -> 0 us
  starting transfers between devices: 20.1 us -> 0 us
  between operations: 14.8 us -> 0.65 us
  other arithmetic: 10.1 us -> 0 us
    unnamed x4 -> x0, waiting for transfers between devices: 72.5 us -> none
    all_gather x2 -> x0, blocking collectives: 46.8 us -> none  [the longest x1 26.8 us: on_device(): lax.all_gather(filter_second, 'gx', axis=0, tiled=True)]
    pallas_call x0 -> x1, Pallas kernels: none -> 45.2 us  [fused(): pl.pallas_call(functools.partial(kernel, n), out_shape=(jax.ShapeDtypeStr...]
    reshape x18 -> x0, local copies, waits for them, and re-layouts: 31.4 us -> none  [filter_from_inputs(): window(stacked, 1, shift_x, shift_y, x_cells, y_cells)]
    dot_general x36 -> x0, matrix products: 26 us -> none  [the longest x18 18.7 us: filter_from_inputs(): lax.dot_general(piece, flat_grads, (((0,), (0,)), ((), ())), preferred_el...]
    ppermute x8 -> x0, starting transfers between devices: 20.1 us -> none  [the longest x4 14.5 us: with_halo(): lax.ppermute(lax.slice_in_dim(block, block.shape[dim] - width, None, axis...]
    slice x12 -> x0, local copies, waits for them, and re-layouts: 12.5 us -> none  [the longest x4 7.85 us: window(): return stacked[start_x:start_x + x_cells, start_y:start_y + y_cells]]
    transpose x20 -> x0, local copies, waits for them, and re-layouts: 5.49 us -> none  [back_data(): jnp.transpose(kernel[shift_x + 1, shift_y + 1], (0, 2, 1))]
  transfers between devices with their start and end apart: 10 -> 0, of which waited for: 2 -> 0; matrix products, arithmetic and copies ran while one was open for 35% -> 0% of each run, Pallas kernels for 0% -> 0%
where the time goes in v1:
time: 49.3 us; the launch traced here: 49.1 us
  Pallas kernels  45.2 us (92%)
  local copies, waits for them, and re-layouts  3.29 us (7%)
  between operations  0.65 us (1%)
    pallas_call x1, Pallas kernels, fused(): pl.pallas_call(functools.partial(kernel, n), out_shape=(jax.ShapeDtypeStr...  45.2 us
    unnamed x7, local copies, waits for them, and re-layouts  3.29 us

profile of v1, /device:TPU:0, one launch (start us, length us, event | category | flops | bytes accessed | tf_op | source)
XLA Modules:
  0.0 49.1 jit_solution(1878014990131267813)
XLA Ops:
  0.6 45.2 %shard_map.85 = (bf16[2,4,128,128]{3,2,1,0:T(8,128)(2,1)}, f32[27,8,128]{2,1,0:T(8,128)}, f32[27,8,128]{2,1,0:T(8,128)}) custom-call(bf16[2,4,128,128]{3,2,1,0:T(8,128)(2,1)} %go.1, bf16[2,4,128,128]{3,2,1,0:T(8,128)(2,1)} %xin.1, bf16[2,4,128,128]{3,2,1,0:T(8,128)(2,1)} %p1.1, bf16[2,4,128,128]{3,2,1,0:T(8,128)(2,1)} %p2.1, bf16[27,8,128]{2,1,0:T(8,128)(2,1)} %bitcast.6, ...), custom_call_target="tpu_custom_call" | custom-call | tf_op jit(solution)/shard_map/pallas_call | solution.py:424
  45.8 0.0 copy-start.1
  45.8 1.7 %copy.12 = bf16[2,4,128,128]{3,2,1,0:T(8,128)(2,1)} copy(bf16[2,4,128,128]{3,2,1,0:T(8,128)(2,1)} %get-tuple-element.12) | data formatting | bytes 524288
  47.5 0.0 copy-done.1
  47.5 0.0 copy-start
  47.5 0.6 %copy.13 = f32[216,128]{1,0:T(8,128)} copy(f32[216,128]{1,0:T(8,128)S(1)} %bitcast.5) | data formatting | bytes 221184
  48.2 0.3 copy-done
  48.5 0.6 %copy.14 = f32[216,128]{1,0:T(8,128)} copy(f32[216,128]{1,0:T(8,128)S(1)} %bitcast.4) | data formatting | bytes 221184
Async XLA Ops:
  45.8 1.7 %copy-start.1 = (f32[27,8,128]{2,1,0:T(8,128)S(1)}, f32[27,8,128]{2,1,0:T(8,128)}, u32[]{:S(2)}) copy-start(f32[27,8,128]{2,1,0:T(8,128)} %get-tuple-element.7) | copy-start | bytes 331780
  47.5 0.9 %copy-start = (f32[27,8,128]{2,1,0:T(8,128)S(1)}, f32[27,8,128]{2,1,0:T(8,128)}, u32[]{:S(2)}) copy-start(f32[27,8,128]{2,1,0:T(8,128)} %get-tuple-element.8) | copy-start | bytes 331780

commit v2 on v1

--- a/solution.py
+++ b/solution.py
@@ -121,7 +121,7 @@
 def kernel(
     n, go, xin, p1, p2, f1, f2, gin, own1, own2,
     fbuf, wbuf, gext, abuf, ahalo, sat, gcat, slope, part, s1, r1, s2, r2, s3, r3,
-    halo_s, halo_r, agz_s, agz_r, agx_s, agx_r, agc_s, agc_r,
+    halo_s, halo_r, agz_s, agz_r, agx_s, agx_r, agy_s, agy_r, agc_s, agc_r,
     rs1_s, rs1_r, rs2_s, rs2_r, rs3_s, rs3_r,
 ):
     xs, ys, zs, ch = go.shape
@@ -146,15 +146,17 @@
     def behind(d):
         return lax.rem(top + hi - d, hi)
 
+    lead = core == group
     sent = []
 
-    def push(src, dst, send, recv, target):
+    def push(src, dst, send, recv, target, plane=group, keep=True):
         copy = pltpu.make_async_remote_copy(
             src_ref=src, dst_ref=dst, send_sem=send, recv_sem=recv,
-            device_id=(group, target), device_id_type=MESH,
+            device_id=(plane, target), device_id_type=MESH,
         )
         copy.start()
-        sent.append(copy)
+        if keep:
+            sent.append(copy)
 
     def arrive(dst, send, recv):
         pltpu.make_async_remote_copy(
@@ -167,30 +169,56 @@
     peers += [owner(ahead(d), mid, core) for d in range(1, hi)]
     for peer in peers:
         pl.semaphore_signal(barrier, inc=1, device_id=(group, peer), device_id_type=MESH)
-    pl.semaphore_wait(barrier, len(peers))
+    pl.semaphore_signal(barrier, inc=1, device_id=(1 - group, me), device_id_type=MESH)
+    pl.semaphore_wait(barrier, len(peers) + 1)
 
     filters = (f2, f1)
 
     def gather_own(f):
         mine = fbuf.at[f, chunk(top, mid, core)]
-        for d in range(1, hi):
-            push(filters[f], mine, agz_s.at[f, d], agz_r.at[f, d], owner(ahead(d), mid, core))
-        push(filters[f], mine, agx_s.at[f, 0], agx_r.at[f, 0], across)
-        push(filters[f], mine, agc_s.at[f, 0], agc_r.at[f, 0], partner)
-        fbuf[f, chunk(top, mid, core)] = filters[f][...]
+        src = filters[f]
+        push(src, mine, agc_s.at[f, 0], agc_r.at[f, 0], partner)
+
+        @pl.when(lead)
+        def _():
+            for d in range(1, hi):
+                push(
+                    src, mine, agz_s.at[f, d], agz_r.at[f, d],
+                    owner(ahead(d), mid, core), keep=False,
+                )
+            push(src, mine, agx_s.at[f, 0], agx_r.at[f, 0], across, keep=False)
+
+        fbuf[f, chunk(top, mid, core)] = src[...]
+
+    def hand_on(f, got, k):
+        push(got, got, agy_s.at[f, k], agy_r.at[f, k], me, 1 - group, False)
+        push(got, got, agc_s.at[f, k], agc_r.at[f, k], partner, keep=False)
 
     def gather_top(f):
-        for d in range(1, hi):
-            got = fbuf.at[f, chunk(behind(d), mid, core)]
-            arrive(got, agz_s.at[f, d], agz_r.at[f, d])
-            push(got, got, agx_s.at[f, d], agx_r.at[f, d], across)
-            push(got, got, agc_s.at[f, d], agc_r.at[f, d], partner)
+        @pl.when(lead)
+        def _():
+            for d in range(1, hi):
+                got = fbuf.at[f, chunk(behind(d), mid, core)]
+                arrive(got, agz_s.at[f, d], agz_r.at[f, d])
+                push(got, got, agx_s.at[f, d], agx_r.at[f, d], across, keep=False)
+                hand_on(f, got, d)
 
     def gather_mid(f):
-        for d in range(hi):
-            got = fbuf.at[f, chunk(behind(d), 1 - mid, core)]
-            arrive(got, agx_s.at[f, d], agx_r.at[f, d])
-            push(got, got, agc_s.at[f, hi + d], agc_r.at[f, hi + d], partner)
+        @pl.when(lead)
+        def _():
+            for d in range(hi):
+                got = fbuf.at[f, chunk(behind(d), 1 - mid, core)]
+                arrive(got, agx_s.at[f, d], agx_r.at[f, d])
+                hand_on(f, got, hi + d)
+
+    def gather_follow(f):
+        @pl.when(jnp.logical_not(lead))
+        def _():
+            for k in range(1, 2 * hi):
+                which = mid if k < hi else 1 - mid
+                got = fbuf.at[f, chunk(behind(k % hi), which, core)]
+                arrive(got, agy_s.at[f, k], agy_r.at[f, k])
+                push(got, got, agc_s.at[f, k], agc_r.at[f, k], partner, keep=False)
 
     def gather_core(f):
         for m in range(2):
@@ -252,13 +280,20 @@
     def saved_halo(h, s, block):
         return halo_copy(h, block.at[0], block.at[xs - 1], ahalo.at[s, 0], ahalo.at[s, 1])
 
+    def keep_shifts(f, x, y, value):
+        for c in (-1, 0, 1):
+            gcat[f, x + 1, y + 1, :, (c + 1) * ch : (c + 2) * ch] = shift_z(value, c).astype(
+                jnp.bfloat16
+            )
+
     def keep_grad(f, x, y, value):
         gext[f, x + 1, y + 1] = value.astype(jnp.bfloat16)
-        start = pl.multiple_of((x * ys + y) * zs, zs)
-        for c in (-1, 0, 1):
-            gcat[f, pl.ds(start, zs), (c + 1) * ch : (c + 2) * ch] = shift_z(value, c).astype(
-                jnp.bfloat16
-            )
+        keep_shifts(f, x, y, value)
+
+    def halo_shifts(f):
+        for x in (-1, xs):
+            for y in range(ys):
+                keep_shifts(f, x, y, gext[f, x + 1, y + 1].astype(jnp.float32))
 
     def turn(s, layer, block):
         for y in range(ys):
@@ -275,7 +310,8 @@
                 ],
                 axis=0,
             )
-            out = jnp.dot(lhs, gcat[s], preferred_element_type=jnp.float32)
+            rhs = gcat[s, 1 : xs + 1, 1 : ys + 1].reshape(xs * ys * zs, 3 * ch)
+            out = jnp.dot(lhs, rhs, preferred_element_type=jnp.float32)
             per = ch // sub
             for b in range(3):
                 for c in range(3):
@@ -284,6 +320,19 @@
                         b * ch : (b + 1) * ch, c * ch : (c + 1) * ch
                     ].reshape(per, sub, ch)
 
+    def filter_terms_halo(s):
+        lhs = jnp.concatenate([sat[s, x + 1, :, zs : (ys + 1) * zs] for x in range(xs)], axis=1)
+        per = ch // sub
+        for a in (0, -1, 1):
+            for b in (-1, 0, 1):
+                rhs = gcat[s, 1 - a : 1 - a + xs, 1 - b : 1 - b + ys].reshape(
+                    xs * ys * zs, 3 * ch
+                )
+                out = jnp.dot(lhs, rhs, preferred_element_type=jnp.float32)
+                for c in range(3):
+                    at = (9 * (a + 1) + 3 * (b + 1) + c) * per
+                    part[s, at : at + per] = out[:, c * ch : (c + 1) * ch].reshape(per, sub, ch)
+
     def scatter_core(s):
         for m in range(2):
             which = 1 - mid if m == 0 else mid
@@ -293,11 +342,12 @@
 
     def scatter_mid(s):
         arrive(r1.at[s, 0], rs1_s.at[s, 0], rs1_r.at[s, 0])
-        for t in range(hi):
+        for d in [*range(1, hi), 0]:
+            t = ahead(d)
             s2[s, t] = (
                 part[s, chunk(t, 1 - mid, core)] + r1[s, 0, t].astype(jnp.float32)
             ).astype(jnp.bfloat16)
-        push(s2.at[s], r2.at[s], rs2_s.at[s], rs2_r.at[s], across)
+            push(s2.at[s, t], r2.at[s, t], rs2_s.at[s, d], rs2_r.at[s, d], across)
 
     def total(s, t):
         return (
@@ -308,8 +358,8 @@
 
     def scatter_top(s):
         arrive(r1.at[s, 1], rs1_s.at[s, 1], rs1_r.at[s, 1])
-        arrive(r2.at[s], rs2_s.at[s], rs2_r.at[s])
         for d in range(1, hi):
+            arrive(r2.at[s, ahead(d)], rs2_s.at[s, d], rs2_r.at[s, d])
             s3[s, d] = total(s, ahead(d)).astype(jnp.bfloat16)
             push(
                 s3.at[s, d], r3.at[s, d], rs3_s.at[s, d], rs3_r.at[s, d],
@@ -317,6 +367,7 @@
             )
 
     def scatter_end(s, out):
+        arrive(r2.at[s, top], rs2_s.at[s, 0], rs2_r.at[s, 0])
         value = total(s, top)
         for d in range(1, hi):
             arrive(r3.at[s, d], rs3_s.at[s, d], rs3_r.at[s, d])
@@ -349,6 +400,7 @@
         for x in range(xs + 2):
             for y in (0, ys + 1):
                 gext[f, x, y] = jnp.zeros((zs, ch), jnp.bfloat16)
+                gcat[f, x, y] = jnp.zeros((zs, 3 * ch), jnp.bfloat16)
                 sat[f, x, :, y * zs : (y + 1) * zs] = jnp.zeros((ch, zs), jnp.bfloat16)
 
     @pl.loop(0, xs * ys)
@@ -360,48 +412,67 @@
         abuf[x, y] = act.astype(jnp.bfloat16)
         slope[x, y] = slope_one
 
-    halo_act = saved_halo(0, 0, abuf)
     halo_two = grad_halo(1, 0)
     gather_top(0)
-    halo_in = saved_halo(2, 1, xin)
-    gather_own(1)
+    halo_in = saved_halo(0, 0, xin)
     for x in range(xs):
         turn(0, x + 1, abuf[x])
         turn(1, x + 1, xin[x])
     gather_mid(0)
-    halo_wait(halo_act)
-    turn(0, 0, ahalo[0, 0])
-    turn(0, xs + 1, ahalo[0, 1])
-    filter_terms(0)
+    gather_own(1)
+    gather_follow(0)
+    halo_wait(halo_two)
+    halo_shifts(0)
+    filter_terms_halo(0)
     scatter_core(0)
+    gather_core(0)
     gather_top(1)
-    gather_core(0)
-    halo_wait(halo_two)
     scatter_mid(0)
     for x in range(xs):
         for y, value in enumerate(layer_back(0, x)):
             keep_grad(1, x, y, value * slope[x, y])
-    halo_one = grad_halo(3, 1)
-    gather_mid(1)
+    halo_one = grad_halo(2, 1)
     halo_wait(halo_in)
-    turn(1, 0, ahalo[1, 0])
-    turn(1, xs + 1, ahalo[1, 1])
+    turn(1, 0, ahalo[0, 0])
+    turn(1, xs + 1, ahalo[0, 1])
     filter_terms(1)
     scatter_core(1)
+    gather_mid(1)
     scatter_top(0)
+    scatter_mid(1)
+    gather_follow(1)
+    scatter_top(1)
     gather_core(1)
-    scatter_mid(1)
     halo_wait(halo_one)
     for x in range(xs):
         for y, value in enumerate(layer_back(1, x)):
             gin[x, y] = value.astype(jnp.bfloat16)
-        if x == 0:
-            scatter_top(1)
     scatter_end(0, own2)
     scatter_end(1, own1)
     for copy in sent:
         copy.wait_send()
-    for halo in (halo_act, halo_two, halo_in, halo_one):
+
+    def left(f, send):
+        pltpu.make_async_remote_copy(
+            src_ref=filters[f], dst_ref=filters[f], send_sem=send, recv_sem=agc_r.at[f, 0],
+            device_id=(group, partner), device_id_type=MESH,
+        ).wait_send()
+
+    for f in range(2):
+        for k in range(1, 2 * hi):
+            left(f, agc_s.at[f, k])
+
+    @pl.when(lead)
+    def _():
+        for f in range(2):
+            for d in range(1, hi):
+                left(f, agz_s.at[f, d])
+            for d in range(hi):
+                left(f, agx_s.at[f, d])
+            for k in range(1, 2 * hi):
+                left(f, agy_s.at[f, k])
+
+    for halo in (halo_two, halo_in, halo_one):
 
         @pl.when(me > 0)
         def _():
@@ -416,7 +487,7 @@
     n = lax.axis_size("gx")
     xs, ys, zs, ch = grad_out.shape
     rows = filter_first.shape[0]
-    if rows % sub or n % 4 or n < 8:
+    if rows % sub or n % 4 or n < 8 or lax.axis_size("groups") != 2:
         return on_device(grad_out, inputs, pre_first, pre_second, filter_first, filter_second)
     units, hi, bf = rows // sub, n // 4, jnp.bfloat16
     dma = pltpu.SemaphoreType.DMA
@@ -435,9 +506,9 @@
             pltpu.VMEM((2, 3 * ch, 9 * ch), bf),
             pltpu.VMEM((2, xs + 2, ys + 2, zs, ch), bf),
             pltpu.VMEM((xs, ys, zs, ch), bf),
-            pltpu.VMEM((2, 2, ys, zs, ch), bf),
+            pltpu.VMEM((1, 2, ys, zs, ch), bf),
             pltpu.VMEM((2, xs + 2, ch, (ys + 2) * zs), bf),
-            pltpu.VMEM((2, xs * ys * zs, 3 * ch), bf),
+            pltpu.VMEM((2, xs + 2, ys + 2, zs, 3 * ch), bf),
             pltpu.VMEM((xs, ys, zs, ch), jnp.float32),
             pltpu.VMEM((2, n * units, sub, ch), jnp.float32),
             pltpu.VMEM((2, 2, hi) + piece, bf),
@@ -446,12 +517,13 @@
             pltpu.VMEM((2, hi) + piece, bf),
             pltpu.VMEM((2, hi) + piece, bf),
             pltpu.VMEM((2, hi) + piece, bf),
-            dma((4, 2)), dma((4, 2)),
+            dma((3, 2)), dma((3, 2)),
             dma((2, hi)), dma((2, hi)),
             dma((2, hi)), dma((2, hi)),
             dma((2, 2 * hi)), dma((2, 2 * hi)),
+            dma((2, 2 * hi)), dma((2, 2 * hi)),
             dma((2, 2)), dma((2, 2)),
-            dma((2,)), dma((2,)),
+            dma((2, hi)), dma((2, hi)),
             dma((2, hi)), dma((2, hi)),
         ],
         compiler_params=pltpu.CompilerParams(collective_id=0, has_side_effects=True),

time: 49.3 us -> 45.6 us (0.925)
  Pallas kernels: 45.2 us -> 41.5 us
    pallas_call x1, Pallas kernels: 45.2 us -> 41.5 us  [fused(): pl.pallas_call(functools.partial(kernel, n), out_shape=(jax.ShapeDtypeStr...]
where the time goes in v2:
time: 45.6 us; the launch traced here: 45.4 us
  Pallas kernels  41.5 us (91%)
  local copies, waits for them, and re-layouts  3.29 us (7%)
  between operations  0.65 us (1%)
    pallas_call x1, Pallas kernels, fused(): pl.pallas_call(functools.partial(kernel, n), out_shape=(jax.ShapeDtypeStr...  41.5 us
    unnamed x7, local copies, waits for them, and re-layouts  3.29 us

profile of v2, /device:TPU:0, one launch (start us, length us, event | category | flops | bytes accessed | tf_op | source)
XLA Modules:
  0.0 45.4 jit_solution(12098550588664337265)
XLA Ops:
  0.6 41.5 %shard_map.85 = (bf16[2,4,128,128]{3,2,1,0:T(8,128)(2,1)}, f32[27,8,128]{2,1,0:T(8,128)}, f32[27,8,128]{2,1,0:T(8,128)}) custom-call(bf16[2,4,128,128]{3,2,1,0:T(8,128)(2,1)} %go.1, bf16[2,4,128,128]{3,2,1,0:T(8,128)(2,1)} %xin.1, bf16[2,4,128,128]{3,2,1,0:T(8,128)(2,1)} %p1.1, bf16[2,4,128,128]{3,2,1,0:T(8,128)(2,1)} %p2.1, bf16[27,8,128]{2,1,0:T(8,128)(2,1)} %bitcast.6, ...), custom_call_target="tpu_custom_call" | custom-call | tf_op jit(solution)/shard_map/pallas_call | solution.py:495
  42.1 0.0 copy-start.1
  42.1 1.7 %copy.12 = bf16[2,4,128,128]{3,2,1,0:T(8,128)(2,1)} copy(bf16[2,4,128,128]{3,2,1,0:T(8,128)(2,1)} %get-tuple-element.12) | data formatting | bytes 524288
  43.8 0.0 copy-done.1
  43.8 0.0 copy-start
  43.8 0.6 %copy.13 = f32[216,128]{1,0:T(8,128)} copy(f32[216,128]{1,0:T(8,128)S(1)} %bitcast.5) | data formatting | bytes 221184
  44.5 0.3 copy-done
  44.8 0.6 %copy.14 = f32[216,128]{1,0:T(8,128)} copy(f32[216,128]{1,0:T(8,128)S(1)} %bitcast.4) | data formatting | bytes 221184
Async XLA Ops:
  42.1 1.7 %copy-start.1 = (f32[27,8,128]{2,1,0:T(8,128)S(1)}, f32[27,8,128]{2,1,0:T(8,128)}, u32[]{:S(2)}) copy-start(f32[27,8,128]{2,1,0:T(8,128)} %get-tuple-element.7) | copy-start | bytes 331780
  43.8 0.9 %copy-start = (f32[27,8,128]{2,1,0:T(8,128)S(1)}, f32[27,8,128]{2,1,0:T(8,128)}, u32[]{:S(2)}) copy-start(f32[27,8,128]{2,1,0:T(8,128)} %get-tuple-element.8) | copy-start | bytes 331780

commit v3 on v2

--- a/solution.py
+++ b/solution.py
@@ -174,12 +174,15 @@
 
     filters = (f2, f1)
 
+    def when_relay(f):
+        return pl.when(lead) if f else lambda run: run()
+
     def gather_own(f):
         mine = fbuf.at[f, chunk(top, mid, core)]
         src = filters[f]
         push(src, mine, agc_s.at[f, 0], agc_r.at[f, 0], partner)
 
-        @pl.when(lead)
+        @when_relay(f)
         def _():
             for d in range(1, hi):
                 push(
@@ -191,11 +194,12 @@
         fbuf[f, chunk(top, mid, core)] = src[...]
 
     def hand_on(f, got, k):
-        push(got, got, agy_s.at[f, k], agy_r.at[f, k], me, 1 - group, False)
+        if f:
+            push(got, got, agy_s.at[f, k], agy_r.at[f, k], me, 1 - group, False)
         push(got, got, agc_s.at[f, k], agc_r.at[f, k], partner, keep=False)
 
     def gather_top(f):
-        @pl.when(lead)
+        @when_relay(f)
         def _():
             for d in range(1, hi):
                 got = fbuf.at[f, chunk(behind(d), mid, core)]
@@ -204,7 +208,7 @@
                 hand_on(f, got, d)
 
     def gather_mid(f):
-        @pl.when(lead)
+        @when_relay(f)
         def _():
             for d in range(hi):
                 got = fbuf.at[f, chunk(behind(d), 1 - mid, core)]
@@ -372,7 +376,7 @@
         for d in range(1, hi):
             arrive(r3.at[s, d], rs3_s.at[s, d], rs3_r.at[s, d])
             value = value + r3[s, d].astype(jnp.float32)
-        out[...] = value * (1.0 / math.sqrt(xs * n * ys * zs))
+        out[...] = value
 
     def layer_back(f, x):
         lhs = jnp.concatenate(
@@ -395,6 +399,8 @@
         return rows
 
     gather_own(0)
+    halo_in = saved_halo(0, 0, xin)
+    gather_own(1)
 
     for f in range(2):
         for x in range(xs + 2):
@@ -414,13 +420,10 @@
 
     halo_two = grad_halo(1, 0)
     gather_top(0)
-    halo_in = saved_halo(0, 0, xin)
     for x in range(xs):
         turn(0, x + 1, abuf[x])
         turn(1, x + 1, xin[x])
     gather_mid(0)
-    gather_own(1)
-    gather_follow(0)
     halo_wait(halo_two)
     halo_shifts(0)
     filter_terms_halo(0)
@@ -431,22 +434,22 @@
     for x in range(xs):
         for y, value in enumerate(layer_back(0, x)):
             keep_grad(1, x, y, value * slope[x, y])
-    halo_one = grad_halo(2, 1)
     halo_wait(halo_in)
     turn(1, 0, ahalo[0, 0])
     turn(1, xs + 1, ahalo[0, 1])
     filter_terms(1)
     scatter_core(1)
+    scatter_mid(1)
+    halo_one = grad_halo(2, 1)
     gather_mid(1)
     scatter_top(0)
-    scatter_mid(1)
     gather_follow(1)
     scatter_top(1)
     gather_core(1)
     halo_wait(halo_one)
     for x in range(xs):
         for y, value in enumerate(layer_back(1, x)):
-            gin[x, y] = value.astype(jnp.bfloat16)
+            gin[x, y] = value
     scatter_end(0, own2)
     scatter_end(1, own1)
     for copy in sent:
@@ -462,15 +465,17 @@
         for k in range(1, 2 * hi):
             left(f, agc_s.at[f, k])
 
-    @pl.when(lead)
-    def _():
-        for f in range(2):
+    for f in range(2):
+
+        @when_relay(f)
+        def _():
             for d in range(1, hi):
                 left(f, agz_s.at[f, d])
             for d in range(hi):
                 left(f, agx_s.at[f, d])
-            for k in range(1, 2 * hi):
-                left(f, agy_s.at[f, k])
+            if f:
+                for k in range(1, 2 * hi):
+                    left(f, agy_s.at[f, k])
 
     for halo in (halo_two, halo_in, halo_one):
 
@@ -495,7 +500,7 @@
     gin, own1, own2 = pl.pallas_call(
         functools.partial(kernel, n),
         out_shape=(
-            jax.ShapeDtypeStruct(grad_out.shape, bf),
+            jax.ShapeDtypeStruct(grad_out.shape, jnp.float32),
             jax.ShapeDtypeStruct(piece, jnp.float32),
             jax.ShapeDtypeStruct(piece, jnp.float32),
         ),
@@ -531,7 +536,8 @@
         grad_out, inputs, pre_first, pre_second,
         filter_first.reshape(piece), filter_second.reshape(piece),
     )
-    return gin, own1.reshape(rows, ch), own2.reshape(rows, ch)
+    scale = 1.0 / math.sqrt(xs * n * ys * zs)
+    return gin.astype(bf), own1.reshape(rows, ch) * scale, own2.reshape(rows, ch) * scale
 
 
 def solution(mesh):

time: 45.6 us -> 43.9 us (0.963)
  local copies, waits for them, and re-layouts: 3.29 us -> 0.01 us
  other arithmetic: 0 us -> 2.53 us
  Pallas kernels: 41.5 us -> 40.5 us
    unnamed x7 -> x4, local copies, waits for them, and re-layouts: 3.29 us -> 0.01 us
    convert_element_type x0 -> x1, other arithmetic: none -> 1.83 us  [fused(): gin.astype(bf)]
    pallas_call x1, Pallas kernels: 41.5 us -> 40.5 us  [fused(): pl.pallas_call(functools.partial(kernel, n), out_shape=(jax.ShapeDtypeStr...]
    mul x0 -> x1, other arithmetic: none -> 0.7 us  [fused(): own2.reshape(rows, ch) * scale]
where the time goes in v3:
time: 43.9 us; the launch traced here: 43.7 us
  Pallas kernels  40.5 us (92%)
  other arithmetic  2.53 us (6%)
  between operations  0.66 us (2%)
    pallas_call x1, Pallas kernels, fused(): pl.pallas_call(functools.partial(kernel, n), out_shape=(jax.ShapeDtypeStr...  40.5 us
    convert_element_type x1, other arithmetic, fused(): gin.astype(bf)  1.83 us

profile of v3, /device:TPU:0, one launch (start us, length us, event | category | flops | bytes accessed | tf_op | source)
XLA Modules:
  0.0 43.7 jit_solution(12780278445871304521)
XLA Ops:
  0.6 40.5 %shard_map.85 = (f32[2,4,128,128]{3,2,1,0:T(8,128)}, f32[27,8,128]{2,1,0:T(8,128)}, f32[27,8,128]{2,1,0:T(8,128)}) custom-call(bf16[2,4,128,128]{3,2,1,0:T(8,128)(2,1)} %go.1, bf16[2,4,128,128]{3,2,1,0:T(8,128)(2,1)} %xin.1, bf16[2,4,128,128]{3,2,1,0:T(8,128)(2,1)} %p1.1, bf16[2,4,128,128]{3,2,1,0:T(8,128)(2,1)} %p2.1, bf16[27,8,128]{2,1,0:T(8,128)(2,1)} %bitcast.6, ...), custom_call_target="tpu_custom_call" | custom-call | tf_op jit(solution)/shard_map/pallas_call | solution.py:500
  41.1 0.0 copy-start
  41.2 0.0 copy-start.1
  41.2 1.8 %convert_element_type.3 = bf16[2,4,128,128]{3,2,1,0:T(8,128)(2,1)} convert(f32[2,4,128,128]{3,2,1,0:T(8,128)} %get-tuple-element.6) | non-fusion elementwise | flops 131072 | bytes 786432 | tf_op jit(solution)/shard_map/convert_element_type | solution.py:540
  43.0 0.0 copy-done
  43.0 0.0 copy-done.1
  43.0 0.7 %multiply_bitcast_fusion = (f32[216,128]{1,0:T(8,128)}, f32[216,128]{1,0:T(8,128)}) fusion(f32[27,8,128]{2,1,0:T(8,128)S(1)} %copy-done.1, f32[27,8,128]{2,1,0:T(8,128)S(1)} %copy-done), kind=kLoop, calls=%fused_computation | loop fusion | flops 55296 | bytes 442368 | tf_op jit(solution)/shard_map/mul | solution.py:540
Async XLA Ops:
  41.1 1.8 %copy-start = (f32[27,8,128]{2,1,0:T(8,128)S(1)}, f32[27,8,128]{2,1,0:T(8,128)}, u32[]{:S(2)}) copy-start(f32[27,8,128]{2,1,0:T(8,128)} %get-tuple-element.7) | copy-start | bytes 331780
  41.2 1.8 %copy-start.1 = (f32[27,8,128]{2,1,0:T(8,128)S(1)}, f32[27,8,128]{2,1,0:T(8,128)}, u32[]{:S(2)}) copy-start(f32[27,8,128]{2,1,0:T(8,128)} %get-tuple-element.8) | copy-start | bytes 331780
